TPU v7x, 32 devices: a whole 2x2x4 slice. The times are simulated.
32 devices in a mesh: grp: 2 (over x), seq: 8 (over z, y), head: 2 (over core).
Axes of the slice: x: 2, y: 2, z: 4, core: 2. Of those that a mesh axis runs over, the one named last changes fastest.
Arguments:
- q_nope: bfloat16 [8, 128, 128], P('grp', ('seq', 'head')), parts along dimension 0, may hold values from -6 to 6
- q_rope: bfloat16 [8, 128, 64], P('grp', ('seq', 'head')), parts along dimension 0, may hold values from -150 to 150
- w_uk: bfloat16 [128, 128, 512], P(('seq', 'head')), may hold values from -0.5 to 0.5
- w_uv: bfloat16 [128, 512, 128], P(('seq', 'head')), may hold values from -1 to 1
- cache: bfloat16 [8, 4096, 576], P('grp', 'seq'), parts along dimension 0, may hold values from -12 to 12
- lengths: int32 [8], P('grp'), parts along dimension 0, may hold values from 2048 to 4096, as said below
- selected: int32 [8, 8, 32], P('grp'), parts along dimension 0, may hold values from 0 to 63, as said below
Outputs:
- attended: bfloat16 [8, 128, 128], P('grp', ('seq', 'head')), parts along dimension 0
- bounds: float32 [8, 8, 64], P('grp', None, 'seq'), parts along dimension 0
There are 2 independent parts, one for each index of `grp`. A program takes and returns all parts, laid end to end along the dimension named above; an argument that names none is the same for every part. Nothing has to cross between parts.
Inputs may be any that keep to these rules, and one draw needn't show every extreme that they name: `lengths`: some request has exactly 4096 cached tokens; every request has 2048 or more. `selected`: for each request and head group the 32 page numbers are distinct and below ceil(lengths[r] / 64); page 0 and the page of the request's last cached token are always among them.
All inputs are finite; a program needn't handle non-finite values.
Results may differ from a plain program's by a relative error of at most 0.0065.
Values may be sent and summed in bfloat16 or wider, within the bound.
A program may use at most 64 MiB of HBM per device.

v0:
```python
import jax
import jax.numpy as jnp
from jax import lax
from jax.sharding import PartitionSpec as P

GH = 16
PAGE = 64


def local(q_nope, q_rope, w_uk, w_uv, cache, lengths, selected):
    seq_count = lax.axis_size("seq")
    head_count = lax.axis_size("head")
    seq_rank = lax.axis_index("seq")
    head_rank = lax.axis_index("head")
    requests = q_nope.shape[0]
    head_block = q_nope.shape[1]
    latent_width = w_uk.shape[2]
    cache_width = cache.shape[2]
    tokens_here = cache.shape[1]
    pages_here = tokens_here // PAGE
    groups = selected.shape[1]
    softmax_scale = (q_nope.shape[2] + q_rope.shape[2]) ** (-0.5)
    query_latent = jnp.einsum(
        "rhn,hnl->rhl", q_nope, w_uk, preferred_element_type=jnp.float32
    ).astype(jnp.bfloat16)
    absorbed = jnp.concatenate([query_latent, q_rope], axis=2)
    queries = lax.all_gather(absorbed, "seq", axis=1, tiled=True)
    heads_here = head_block * seq_count
    position = jnp.arange(heads_here, dtype=jnp.int32)
    global_head = (
        position // head_block * head_count + head_rank
    ) * head_block + position % head_block
    group_of = global_head // GH
    group_hot = group_of[:, None] == jnp.arange(groups, dtype=jnp.int32)[None, :]
    page_number = seq_rank * pages_here + jnp.arange(pages_here, dtype=jnp.int32)
    token_index = seq_rank * tokens_here + jnp.arange(tokens_here, dtype=jnp.int32).reshape(
        pages_here, PAGE
    )
    live_token = token_index[None] < lengths[:, None, None]
    live_page = live_token[:, :, 0]
    page_blocks = cache.reshape(requests, pages_here, PAGE, cache_width)
    page_low = jnp.min(jnp.where(live_token[..., None], page_blocks, jnp.inf), axis=2).astype(
        jnp.float32
    )
    page_high = jnp.max(jnp.where(live_token[..., None], page_blocks, -jnp.inf), axis=2).astype(
        jnp.float32
    )
    page_low = jnp.where(live_page[..., None], page_low, 0.0)
    page_high = jnp.where(live_page[..., None], page_high, 0.0)
    middle = (page_low + page_high) * 0.5
    spread = (page_high - page_low) * 0.5
    query_float = queries.astype(jnp.float32)
    head_bound = softmax_scale * (
        jnp.einsum("rhd,rpd->rhp", query_float, middle, precision=lax.Precision.HIGHEST)
        + jnp.einsum("rhd,rpd->rhp", jnp.abs(query_float), spread, precision=lax.Precision.HIGHEST)
    )
    group_bound = jnp.max(
        jnp.where(group_hot.T[None, :, :, None], head_bound[:, None, :, :], -1e30), axis=2
    )
    group_bound = lax.pmax(group_bound, "head")
    bounds = jnp.where(live_page[:, None, :], group_bound, 0.0)
    picked = jnp.any(selected[:, :, :, None] == page_number[None, None, None, :], axis=2)
    head_pick = jnp.any(group_hot[None, :, :, None] & picked[:, None, :, :], axis=2)
    scores = (
        jnp.einsum("rhd,rtd->rht", queries, cache, preferred_element_type=jnp.float32)
        * softmax_scale
    )
    scores = scores.reshape(requests, heads_here, pages_here, PAGE)
    scores = jnp.where(live_token[:, None], scores, -1e30)
    page_top = jnp.max(scores, axis=3)
    weights = jnp.where(live_token[:, None], jnp.exp(scores - page_top[..., None]), 0.0).astype(
        jnp.bfloat16
    )
    page_total = jnp.sum(weights.astype(jnp.float32), axis=3)
    page_weighted = jnp.einsum(
        "rhpt,rptl->rhpl",
        weights,
        page_blocks[..., :latent_width],
        preferred_element_type=jnp.float32,
    )
    summit = jnp.max(jnp.where(head_pick, page_top, -1e30), axis=2)
    factor = jnp.where(head_pick, jnp.exp(page_top - summit[..., None]), 0.0)
    total = jnp.sum(factor * page_total, axis=2)
    weighted = jnp.einsum("rhp,rhpl->rhl", factor, page_weighted, precision=lax.Precision.HIGHEST)
    gotten = (
        lax.all_to_all(
            summit.reshape(requests, seq_count, head_block),
            "seq",
            split_axis=1,
            concat_axis=1,
            tiled=True,
        ),
        lax.all_to_all(
            total.reshape(requests, seq_count, head_block),
            "seq",
            split_axis=1,
            concat_axis=1,
            tiled=True,
        ),
        lax.all_to_all(
            weighted.reshape(requests, seq_count, head_block, latent_width),
            "seq",
            split_axis=1,
            concat_axis=1,
            tiled=True,
        ),
    )
    highest = jnp.max(gotten[0], axis=1)
    rescale = jnp.exp(gotten[0] - highest[:, None, :])
    own_total = jnp.sum(rescale * gotten[1], axis=1)
    own_weighted = jnp.sum(rescale[..., None] * gotten[2], axis=1)
    latent_out = (own_weighted / own_total[..., None]).astype(jnp.bfloat16)
    attended = jnp.einsum(
        "rhl,hlv->rhv", latent_out, w_uv, preferred_element_type=jnp.float32
    ).astype(jnp.bfloat16)
    return (attended, bounds)


def solution(mesh):
    placed = (
        P("grp", ("seq", "head"), None),
        P("grp", ("seq", "head"), None),
        P(("seq", "head"), None, None),
        P(("seq", "head"), None, None),
        P("grp", "seq", None),
        P("grp"),
        P("grp", None, None),
    )
    return jax.shard_map(
        local,
        mesh=mesh,
        in_specs=placed,
        out_specs=(P("grp", ("seq", "head"), None), P("grp", None, "seq")),
        check_vma=False,
    )
```

profile of v0, /device:TPU:0, one launch (start us, length us, event | category | flops | bytes accessed | tf_op | source)
XLA Modules:
  0.0 88.1 jit_solution(16813406923026156517)
XLA Ops:
  0.6 0.0 copy-start
  0.7 0.8 copy.102
  1.5 0.4 copy-done
  1.9 0.9 %fusion.3 = bf16[4,8,512]{2,0,1:T(4,128)(2,1)S(1)} fusion(bf16[8,128,512]{2,1,0:T(8,128)(2,1)S(1)} %copy-done, bf16[4,8,128]{2,1,0:T(8,128)(2,1)} %param.7), kind=kOutput, calls=%fused_computation.8 | convolution fusion | flops 4210688 | bytes 1089536 | tf_op jit(solution)/shard_map/rhn,hnl->rhl/dot_general | solution.py:23
  2.8 0.0 copy-start.3
  2.8 0.0 copy-start.4
  2.9 32.7 %all_gather.3 = bf16[4,64,576]{2,0,1:T(4,128)(2,1)S(1)} all-gather(bf16[4,8,576]{2,0,1:T(4,128)(2,1)S(1)} %pad_maximum_fusion), channel_id=1, replica_groups=mesh['grp'=2,'seq'=8,'head'=2] {'seq'}, dimensions={1}, use_global_device_ids=true | all-gather | bytes 331776 | tf_op jit(solution)/shard_map/all_gather | solution.py:27
  35.5 2.2 %convolution_multiply_fusion = f32[4,64,512]{2,1,0:T(8,128)S(1)} fusion(bf16[4,512,576]{1,2,0:T(8,128)(2,1)} %param.11, bf16[4,64,576]{2,0,1:T(4,128)(2,1)S(1)} %all_gather.3), kind=kOutput, calls=%fused_computation.6 | convolution fusion | flops 151126016 | bytes 3178496 | tf_op jit(solution)/shard_map/rhd,rtd->rht/dot_general | solution.py:65
  37.7 0.2 reshape.136
  37.9 0.0 copy-done.3
  38.0 0.7 compare_reduce_fusion
  38.6 0.1 and_reduce_fusion
  38.8 0.0 copy-done.4
  38.8 0.1 broadcast_compare_fusion
  38.9 0.4 fusion.6
  39.2 0.1 reshape.137
  39.3 0.6 copy.105
  39.9 5.6 %all-to-all-start = ((f32[4,8,8]{2,0,1:T(4,128)}), f32[4,8,8]{2,0,1:T(4,128)S(1)}, u32[]{:S(2)}, u32[]{:S(2)}) async-start(f32[4,8,8]{2,0,1:T(4,128)} %copy.105), calls=%async_computation | async-start | bytes 32768 | tf_op jit(solution)/shard_map/all_to_all | solution.py:86
  45.5 0.7 convert_reduce_fusion
  46.2 4.3 %copy.106 = bf16[4,512,576]{2,1,0:T(8,128)(2,1)} copy(bf16[4,512,576]{1,2,0:T(8,128)(2,1)} %param.11) | data formatting | bytes 4718592 | tf_op args[4]
  50.6 0.1 copy.114
  50.7 0.0 copy-start.1
  50.7 2.7 %select_reduce_fusion.1 = (bf16[4,8,576]{2,1,0:T(8,128)(2,1)S(1)}, bf16[4,8,576]{2,1,0:T(8,128)(2,1)S(1)}) fusion(pred[4,8,64]{2,1,0:T(8,128)(4,1)S(1)} %broadcast_compare_fusion, bf16[4,512,576]{2,1,0:T(8,128)(2,1)} %copy.106), kind=kLoop, calls=%fused_computation.3 | loop fusion | flops 4681728 | bytes 2435072 | tf_op jit(solution)/shard_map/reduce_min | solution.py:42
  53.4 0.0 copy-done.1
  53.4 1.0 %convolution_bitcast_fusion = f32[4,64,8,512]{3,1,2,0:T(8,128)S(1)} fusion(bf16[4,8,64,576]{3,2,1,0:T(8,128)(2,1)S(1)} %bitcast.20, f32[4,64,8,64]{3,2,1,0:T(8,128)S(1)} %reshape.136, f32[4,64,8]{1,2,0:T(8,128)S(1)} %fusion.6, pred[4,8,64]{2,1,0:T(8,128)(4,1)S(1)} %broadcast_compare_fusion), kind=kOutput, calls=%fused_computation.4 | convolution fusion | flops 134742016 | bytes 7360512 | tf_op jit(solution)/shard_map/rhpt,rptl->rhpl/dot_general | solution.py:75
  54.4 5.4 %fusion = f32[4,64,1,512]{3,2,1,0:T(1,128)S(1)} fusion(f32[4,64,8,1]{2,3,1,0:T(1,128)S(1)} %copy.114, f32[4,64,8,512]{3,1,2,0:T(8,128)S(1)} %convolution_bitcast_fusion), kind=kOutput, calls=%fused_computation | convolution fusion | flops 12582912 | bytes 4726784 | tf_op jit(solution)/shard_map/rhp,rhpl->rhl/dot_general | solution.py:84
  59.8 0.1 slice_reduce_fusion
  59.9 0.1 reshape.140
  60.0 0.6 copy.108
  60.6 0.0 all-to-all-done
  60.7 6.0 %all-to-all-start.2 = ((f32[4,8,8]{2,0,1:T(4,128)}), f32[4,8,8]{2,0,1:T(4,128)S(1)}, u32[]{:S(2)}, u32[]{:S(2)}) async-start(f32[4,8,8]{2,0,1:T(4,128)} %copy.108), calls=%async_computation.2 | async-start | bytes 32768 | tf_op jit(solution)/shard_map/all_to_all | solution.py:93
  66.7 0.0 copy-start.2
  66.7 0.5 fusion.10
  67.2 0.8 copy.107
  68.0 5.3 %all-to-all-done.2 = f32[4,8,8]{2,0,1:T(4,128)S(1)} async-done(((f32[4,8,8]{2,0,1:T(4,128)}), f32[4,8,8]{2,0,1:T(4,128)S(1)}, u32[]{:S(2)}, u32[]{:S(2)}) %all-to-all-start.2) | async-done | bytes 1056 | tf_op jit(solution)/shard_map/all_to_all | solution.py:93
  73.3 3.5 %all-to-all-start.1 = ((f32[4,8,8,512]{3,2,0,1:T(8,128)}), f32[4,8,8,512]{3,2,0,1:T(8,128)S(1)}, u32[]{:S(2)}, u32[]{:S(2)}) async-start(f32[4,8,8,512]{3,2,0,1:T(8,128)} %copy.107), calls=%async_computation.1 | async-start | bytes 1048576 | tf_op jit(solution)/shard_map/all_to_all | solution.py:100
  76.8 0.8 fusion.4
  77.6 0.1 select_reduce_fusion.2
  77.7 3.4 %pmax.7 = f32[4,8,8]{2,1,0:T(8,128)S(1)} all-reduce(f32[4,8,8]{2,1,0:T(8,128)S(1)} %select_reduce_fusion.2), channel_id=1, replica_groups=mesh['grp'=2,'seq'=8,'head'=2] {'head'}, use_global_device_ids=true, to_apply=%region_12.13 | all-reduce | flops 256 | bytes 2048 | tf_op jit(solution)/shard_map/pmax | solution.py:60
  81.1 0.6 broadcast_select_fusion
  81.8 5.2 %all-to-all-done.1 = f32[4,8,8,512]{3,2,0,1:T(8,128)S(1)} async-done(((f32[4,8,8,512]{3,2,0,1:T(8,128)}), f32[4,8,8,512]{3,2,0,1:T(8,128)S(1)}, u32[]{:S(2)}, u32[]{:S(2)}) %all-to-all-start.1) | async-done | bytes 524320 | tf_op jit(solution)/shard_map/all_to_all | solution.py:100
  87.0 0.1 multiply_reduce_fusion
  87.1 0.1 divide_convert_fusion
  87.2 0.0 copy-done.2
  87.2 0.2 fusion.5
  87.4 0.6 copy.113
  (11 shorter events, 0.2 us)
Async XLA Ops:
  0.6 1.2 %copy-start = (bf16[8,128,512]{2,1,0:T(8,128)(2,1)S(1)}, bf16[8,128,512]{2,1,0:T(8,128)(2,1)}, u32[]{:S(2)}) copy-start(bf16[8,128,512]{2,1,0:T(8,128)(2,1)} %param.9) | copy-start | bytes 3145732
  2.8 35.1 %copy-start.3 = (s32[4,8,32]{2,1,0:T(8,128)S(1)}, s32[4,8,32]{2,1,0:T(8,128)}, u32[]{:S(2)}) copy-start(s32[4,8,32]{2,1,0:T(8,128)} %param.13) | copy-start | bytes 12292
  2.8 36.0 %copy-start.4 = (s32[4]{0:T(128)S(1)}, s32[4]{0:T(128)}, u32[]{:S(2)}) copy-start(s32[4]{0:T(128)} %param.12) | copy-start | bytes 52
  39.9 20.7 %all-to-all-start = ((f32[4,8,8]{2,0,1:T(4,128)}), f32[4,8,8]{2,0,1:T(4,128)S(1)}, u32[]{:S(2)}, u32[]{:S(2)}) async-start(f32[4,8,8]{2,0,1:T(4,128)} %copy.105), calls=%async_computation | async-start | bytes 32768 | tf_op jit(solution)/shard_map/all_to_all | solution.py:86
  50.7 2.7 %copy-start.1 = (bf16[4,512,576]{2,1,0:T(8,128)(2,1)S(1)}, bf16[4,512,576]{2,1,0:T(8,128)(2,1)}, u32[]{:S(2)}) copy-start(bf16[4,512,576]{2,1,0:T(8,128)(2,1)} %copy.106) | copy-start | bytes 7077892
  60.7 12.6 %all-to-all-start.2 = ((f32[4,8,8]{2,0,1:T(4,128)}), f32[4,8,8]{2,0,1:T(4,128)S(1)}, u32[]{:S(2)}, u32[]{:S(2)}) async-start(f32[4,8,8]{2,0,1:T(4,128)} %copy.108), calls=%async_computation.2 | async-start | bytes 32768 | tf_op jit(solution)/shard_map/all_to_all | solution.py:93
  66.7 20.5 %copy-start.2 = (bf16[8,512,128]{2,1,0:T(8,128)(2,1)S(1)}, bf16[8,512,128]{2,1,0:T(8,128)(2,1)}, u32[]{:S(2)}) copy-start(bf16[8,512,128]{2,1,0:T(8,128)(2,1)} %param.10) | copy-start | bytes 3145732
  73.3 13.7 %all-to-all-start.1 = ((f32[4,8,8,512]{3,2,0,1:T(8,128)}), f32[4,8,8,512]{3,2,0,1:T(8,128)S(1)}, u32[]{:S(2)}, u32[]{:S(2)}) async-start(f32[4,8,8,512]{3,2,0,1:T(8,128)} %copy.107), calls=%async_computation.1 | async-start | bytes 1048576 | tf_op jit(solution)/shard_map/all_to_all | solution.py:100
where the time goes:
time: 88.6 us; the launch traced here: 88.1 us
  blocking collectives  36 us (41%)
  starting transfers between devices  15.1 us (17%)
  matrix products  11 us (12%)
  waiting for transfers between devices  10.5 us (12%)
  local copies, waits for them, and re-layouts  8.85 us (10%)
  other arithmetic  5.68 us (6%)
    all_gather x1, blocking collectives, local(): queries = lax.all_gather(absorbed, 'seq', axis=1, tiled=True)  32.7 us
    unnamed x13, local copies, waits for them, and re-layouts  6.15 us
    all_to_all x1, starting transfers between devices, local(): lax.all_to_all(total.reshape(requests, seq_count, head_block), 'seq', spl...  6.01 us
    all_to_all x1, starting transfers between devices, local(): lax.all_to_all(summit.reshape(requests, seq_count, head_block), 'seq', sp...  5.61 us
    dot_general x1, matrix products, local(): jnp.einsum('rhp,rhpl->rhl', factor, page_weighted, precision=lax.Precisio...  5.37 us
    all_to_all x1, waiting for transfers between devices, local(): lax.all_to_all(total.reshape(requests, seq_count, head_block), 'seq', spl...  5.28 us
    all_to_all x1, waiting for transfers between devices, local(): lax.all_to_all(weighted.reshape(requests, seq_count, head_block, latent_w...  5.23 us
    all_to_all x1, starting transfers between devices, local(): lax.all_to_all(weighted.reshape(requests, seq_count, head_block, latent_w...  3.49 us
  transfers between devices with their start and end apart: 3, of which 2 were waited for; matrix products, arithmetic and copies ran while one was open for 20% of the time, Pallas kernels for 0%

commit v1 on v0

--- a/solution.py
+++ b/solution.py
@@ -5,6 +5,19 @@
 
 GH = 16
 PAGE = 64
+
+
+def gather_around(shard, axis, dim):
+    ways = lax.axis_size(axis)
+    up = [(d, (d + 1) % ways) for d in range(ways)]
+    down = [(d, (d - 1) % ways) for d in range(ways)]
+    earlier, later = ([shard], [shard])
+    for _ in range(ways // 2):
+        earlier.append(lax.ppermute(earlier[-1], axis, up))
+    for _ in range((ways - 1) // 2):
+        later.append(lax.ppermute(later[-1], axis, down))
+    line = jnp.concatenate([*earlier[::-1], *later[1:]], axis=dim)
+    return jnp.roll(line, (lax.axis_index(axis) - ways // 2) * shard.shape[dim], axis=dim)
 
 
 def local(q_nope, q_rope, w_uk, w_uv, cache, lengths, selected):
@@ -24,7 +37,7 @@
         "rhn,hnl->rhl", q_nope, w_uk, preferred_element_type=jnp.float32
     ).astype(jnp.bfloat16)
     absorbed = jnp.concatenate([query_latent, q_rope], axis=2)
-    queries = lax.all_gather(absorbed, "seq", axis=1, tiled=True)
+    queries = gather_around(absorbed, "seq", 1)
     heads_here = head_block * seq_count
     position = jnp.arange(heads_here, dtype=jnp.int32)
     global_head = (

time: 88.6 us -> 94.2 us (1.063)
  blocking collectives: 36 us -> 3.36 us
  starting transfers between devices: 15.1 us -> 30 us
  local copies, waits for them, and re-layouts: 8.85 us -> 17.2 us
  matrix products: 11 us -> 16.3 us
  waiting for transfers between devices: 10.5 us -> 15.3 us
  other arithmetic: 5.68 us -> 10.1 us
    all_gather x1 -> x0, blocking collectives: 32.7 us -> none  [local(): queries = lax.all_gather(absorbed, 'seq', axis=1, tiled=True)]
    ppermute x0 -> x7, starting transfers between devices: none -> 15.9 us  [the longest x3 12.9 us: gather_around(): later.append(lax.ppermute(later[-1], axis, down))]
    ppermute x0 -> x7, waiting for transfers between devices: none -> 8.94 us  [the longest x4 8.65 us: gather_around(): earlier.append(lax.ppermute(earlier[-1], axis, up))]
    unnamed x13 -> x37, local copies, waits for them, and re-layouts: 6.15 us -> 13.4 us
    all_to_all x1, waiting for transfers between devices: 5.28 us -> 1.52 us  [local(): lax.all_to_all(total.reshape(requests, seq_count, head_block), 'seq', spl...]
    dot_general x1, matrix products: 1.03 us -> 4.28 us  [local(): jnp.einsum('rhpt,rptl->rhpl', weights, page_blocks[..., :latent_width], p...]
    dot_general x1, matrix products: 5.37 us -> 8.21 us  [local(): jnp.einsum('rhp,rhpl->rhl', factor, page_weighted, precision=lax.Precisio...]
    all_to_all x1, starting transfers between devices: 3.49 us -> 6 us  [local(): lax.all_to_all(weighted.reshape(requests, seq_count, head_block, latent_w...]
  transfers between devices with their start and end apart: 3 -> 10, of which waited for: 2 -> 6; matrix products, arithmetic and copies ran while one was open for 20% -> 33% of each run, Pallas kernels for 0% -> 0%
where the time goes in v1:
time: 94.2 us; the launch traced here: 93.1 us
  starting transfers between devices  30 us (32%)
  local copies, waits for them, and re-layouts  17.2 us (18%)
  matrix products  16.3 us (17%)
  waiting for transfers between devices  15.3 us (16%)
  other arithmetic  10.1 us (11%)
  blocking collectives  3.36 us (4%)
    unnamed x37, local copies, waits for them, and re-layouts  13.4 us
    ppermute x3, starting transfers between devices, gather_around(): later.append(lax.ppermute(later[-1], axis, down))  12.9 us
    ppermute x4, waiting for transfers between devices, gather_around(): earlier.append(lax.ppermute(earlier[-1], axis, up))  8.65 us
    dot_general x1, matrix products, local(): jnp.einsum('rhp,rhpl->rhl', factor, page_weighted, precision=lax.Precisio...  8.21 us
    all_to_all x1, starting transfers between devices, local(): lax.all_to_all(weighted.reshape(requests, seq_count, head_block, latent_w...  6 us
    all_to_all x1, waiting for transfers between devices, local(): lax.all_to_all(weighted.reshape(requests, seq_count, head_block, latent_w...  4.83 us
    all_to_all x1, starting transfers between devices, local(): lax.all_to_all(summit.reshape(requests, seq_count, head_block), 'seq', sp...  4.5 us
    dot_general x1, matrix products, local(): jnp.einsum('rhpt,rptl->rhpl', weights, page_blocks[..., :latent_width], p...  4.28 us
  transfers between devices with their start and end apart: 10, of which 6 were waited for; matrix products, arithmetic and copies ran while one was open for 33% of the time, Pallas kernels for 0%

profile of v1, /device:TPU:0, one launch (start us, length us, event | category | flops | bytes accessed | tf_op | source)
XLA Modules:
  0.0 93.1 jit_solution(16636368182199368681)
XLA Ops:
  0.6 0.0 copy-start
  0.6 1.2 %copy-done = bf16[8,128,512]{2,1,0:T(8,128)(2,1)S(1)} copy-done((bf16[8,128,512]{2,1,0:T(8,128)(2,1)S(1)}, bf16[8,128,512]{2,1,0:T(8,128)(2,1)}, u32[]{:S(2)}) %copy-start) | copy-done | bytes 1048600
  1.9 0.9 %fusion.25 = bf16[8,512,4]{1,2,0:T(4,128)(2,1)S(1)} fusion(bf16[8,128,512]{2,1,0:T(8,128)(2,1)S(1)} %copy-done, bf16[4,8,128]{2,1,0:T(8,128)(2,1)} %param.7), kind=kOutput, calls=%fused_computation.66 | convolution fusion | flops 4194304 | bytes 1089536 | tf_op jit(solution)/shard_map/rhn,hnl->rhl/dot_general | solution.py:36
  2.8 1.3 %pad_maximum_fusion = bf16[4,8,576]{2,1,0:T(8,128)(2,1)} fusion(bf16[4,8,64]{2,1,0:T(8,128)(2,1)} %param.8, bf16[4,8,512]{2,1,0:T(8,128)(2,1)S(1)} %bitcast.23), kind=kLoop, calls=%fused_computation.34 | loop fusion | flops 73728 | bytes 73728 | tf_op jit(solution)/shard_map/concatenate | solution.py:39
  4.1 3.0 %collective-permute-start = (bf16[4,8,576]{2,1,0:T(8,128)(2,1)}, bf16[4,8,576]{2,1,0:T(8,128)(2,1)S(1)}, u32[]{:S(2)}, u32[]{:S(2)}) collective-permute-start(bf16[4,8,576]{2,1,0:T(8,128)(2,1)} %pad_maximum_fusion), channel_id=1, source_target_pairs={{0,2},{2,4},{4,6},{6,8},{8,10},{10,12},{12,14},{14,0},{1,3},{3,5},... | collective-permute-start | bytes 110600 | tf_op jit(solution)/shard_map/ppermute | solution.py:16
  7.1 3.0 %collective-permute-start.4 = (bf16[4,8,576]{2,1,0:T(8,128)(2,1)}, bf16[4,8,576]{2,1,0:T(8,128)(2,1)S(1)}, u32[]{:S(2)}, u32[]{:S(2)}) collective-permute-start(bf16[4,8,576]{2,1,0:T(8,128)(2,1)} %pad_maximum_fusion), channel_id=1, source_target_pairs={{0,14},{2,0},{4,2},{6,4},{8,6},{10,8},{12,10},{14,12},{1,15},{3,1}... | collective-permute-start | bytes 110600 | tf_op jit(solution)/shard_map/ppermute | solution.py:18
  10.2 0.6 iota_compare_fusion
  10.8 0.6 iota_compare_fusion.1
  11.4 4.4 %copy.102 = bf16[4,512,576]{2,1,0:T(8,128)(2,1)} copy(bf16[4,512,576]{1,2,0:T(8,128)(2,1)} %param.11) | data formatting | bytes 4718592 | tf_op args[4]
  15.7 0.9 broadcast_compare_fusion
  16.6 3.1 %select_reduce_fusion.1 = (bf16[4,8,576]{2,1,0:T(8,128)(2,1)}, bf16[4,8,576]{2,1,0:T(8,128)(2,1)}) fusion(pred[4,8,64]{2,1,0:T(8,128)(4,1)S(1)} %broadcast_compare_fusion, bf16[4,512,576]{2,1,0:T(8,128)(2,1)} %copy.102), kind=kLoop, calls=%fused_computation.3 | loop fusion | flops 4681728 | bytes 2435072 | tf_op jit(solution)/shard_map/reduce_min | solution.py:55
  19.8 0.0 collective-permute-done
  19.8 0.0 collective-permute-start.1
  19.8 0.7 compare_reduce_fusion
  20.5 6.0 %collective-permute-done.1 = bf16[4,8,576]{2,1,0:T(8,128)(2,1)S(1)} collective-permute-done((bf16[4,8,576]{2,1,0:T(8,128)(2,1)S(1)}, bf16[4,8,576]{2,1,0:T(8,128)(2,1)S(1)}, u32[]{:S(2)}, u32[]{:S(2)}) %collective-permute-start.1) | collective-permute-done | bytes 36896 | tf_op jit(solution)/shard_map/ppermute | solution.py:16
  26.5 0.0 collective-permute-start.2
  26.5 0.8 and_reduce_fusion
  27.3 0.0 collective-permute-done.4
  27.3 4.8 %collective-permute-start.5 = (bf16[4,8,576]{2,1,0:T(8,128)(2,1)S(1)}, bf16[4,8,576]{2,1,0:T(8,128)(2,1)}, u32[]{:S(2)}, u32[]{:S(2)}) collective-permute-start(bf16[4,8,576]{2,1,0:T(8,128)(2,1)S(1)} %collective-permute-done.4), channel_id=1, source_target_pairs={{0,14},{2,0},{4,2},{6,4},{8,6},{10,8},{12,10},{14,12},{1,15},{3,1}... | collective-permute-start | bytes 110600 | tf_op jit(solution)/shard_map/ppermute | solution.py:18
  32.0 1.2 %collective-permute-done.2 = bf16[4,8,576]{2,1,0:T(8,128)(2,1)} collective-permute-done((bf16[4,8,576]{2,1,0:T(8,128)(2,1)S(1)}, bf16[4,8,576]{2,1,0:T(8,128)(2,1)}, u32[]{:S(2)}, u32[]{:S(2)}) %collective-permute-start.2) | collective-permute-done | bytes 36896 | tf_op jit(solution)/shard_map/ppermute | solution.py:16
  33.3 0.0 collective-permute-start.3
  33.3 0.1 slice_reduce_fusion
  33.4 0.3 collective-permute-done.5
  33.7 5.1 %collective-permute-start.6 = (bf16[4,8,576]{2,1,0:T(8,128)(2,1)}, bf16[4,8,576]{2,1,0:T(8,128)(2,1)S(1)}, u32[]{:S(2)}, u32[]{:S(2)}) collective-permute-start(bf16[4,8,576]{2,1,0:T(8,128)(2,1)} %collective-permute-done.5), channel_id=1, source_target_pairs={{0,14},{2,0},{4,2},{6,4},{8,6},{10,8},{12,10},{14,12},{1,15},{3,1}... | collective-permute-start | bytes 110600 | tf_op jit(solution)/shard_map/ppermute | solution.py:18
  38.8 1.4 %collective-permute-done.3 = bf16[4,8,576]{2,1,0:T(8,128)(2,1)} collective-permute-done((bf16[4,8,576]{2,1,0:T(8,128)(2,1)}, bf16[4,8,576]{2,1,0:T(8,128)(2,1)}, u32[]{:S(2)}, u32[]{:S(2)}) %collective-permute-start.3) | collective-permute-done | bytes 36896 | tf_op jit(solution)/shard_map/ppermute | solution.py:16
  40.3 0.8 constant_dynamic-update-slice_fusion.15
  41.1 0.8 constant_dynamic-update-slice_fusion.14
  41.8 0.8 constant_dynamic-update-slice_fusion.13
  42.7 0.8 constant_dynamic-update-slice_fusion.9
  43.5 0.0 collective-permute-done.6
  43.5 0.8 constant_dynamic-update-slice_fusion.7
  44.3 0.8 constant_dynamic-update-slice_fusion.6
  45.1 0.8 constant_dynamic-update-slice_fusion.5
  45.9 0.8 constant_dynamic-update-slice_fusion.1
  46.7 0.8 copy-done.3
  47.6 1.3 %convolution_multiply_fusion = f32[4,64,512]{2,1,0:T(8,128)} fusion(bf16[4,512,576]{1,2,0:T(8,128)(2,1)S(1)} %copy-done.1, bf16[4,128,576]{2,1,0:T(8,128)(2,1)S(1)} %constant_dynamic-update-slice_fusion, s32[]{:T(128)S(6)} %select_n.79), kind=kOutput, calls=%fused_computation.6 | convolution fusion | flops 151126016 | bytes 3211268 | tf_op jit(solution)/shard_map/rhd,rtd->rht/dot_general | solution.py:78
  48.9 1.2 %reshape.136 = f32[4,64,8,64]{3,2,1,0:T(8,128)S(1)} reshape(f32[4,64,512]{2,1,0:T(8,128)} %convolution_multiply_fusion) | data formatting | bytes 1048576 | tf_op jit(solution)/shard_map/reshape | solution.py:81
  50.1 0.4 fusion.5
  50.5 0.7 convert_reduce_fusion
  51.2 0.1 reshape.140
  51.3 0.6 copy.104
  51.9 3.5 %all-to-all-start.2 = ((f32[4,8,8]{2,0,1:T(4,128)}), f32[4,8,8]{2,0,1:T(4,128)S(1)}, u32[]{:S(2)}, u32[]{:S(2)}) async-start(f32[4,8,8]{2,0,1:T(4,128)} %copy.104), calls=%async_computation.2 | async-start | bytes 32768 | tf_op jit(solution)/shard_map/all_to_all | solution.py:106
  55.5 4.3 %convolution_bitcast_fusion = f32[4,64,8,512]{3,1,2,0:T(8,128)} fusion(bf16[4,8,64,576]{3,2,1,0:T(8,128)(2,1)} %bitcast.21, f32[4,64,8,64]{3,2,1,0:T(8,128)S(1)} %reshape.136, f32[4,64,8]{1,2,0:T(8,128)S(1)} %fusion.5, pred[4,8,64]{2,1,0:T(8,128)(4,1)S(1)} %broadcast_compare_fusion), kind=kOutput, calls=%fused_computation.4 | convolution fusion | flops 134742016 | bytes 6825984 | tf_op jit(solution)/shard_map/rhpt,rptl->rhpl/dot_general | solution.py:88
  59.8 0.1 reshape.137
  59.8 0.6 copy.101
  60.4 0.1 copy.108
  60.5 1.5 %all-to-all-done.2 = f32[4,8,8]{2,0,1:T(4,128)S(1)} async-done(((f32[4,8,8]{2,0,1:T(4,128)}), f32[4,8,8]{2,0,1:T(4,128)S(1)}, u32[]{:S(2)}, u32[]{:S(2)}) %all-to-all-start.2) | async-done | bytes 1056 | tf_op jit(solution)/shard_map/all_to_all | solution.py:106
  62.1 4.5 %all-to-all-start = ((f32[4,8,8]{2,0,1:T(4,128)}), f32[4,8,8]{2,0,1:T(4,128)S(1)}, u32[]{:S(2)}, u32[]{:S(2)}) async-start(f32[4,8,8]{2,0,1:T(4,128)} %copy.101), calls=%async_computation | async-start | bytes 32768 | tf_op jit(solution)/shard_map/all_to_all | solution.py:99
  66.6 8.2 %fusion = f32[4,64,1,512]{3,2,1,0:T(1,128)S(1)} fusion(f32[4,64,8,1]{2,3,1,0:T(1,128)S(1)} %copy.108, f32[4,64,8,512]{3,1,2,0:T(8,128)} %convolution_bitcast_fusion), kind=kOutput, calls=%fused_computation | convolution fusion | flops 12582912 | bytes 4726784 | tf_op jit(solution)/shard_map/rhp,rhpl->rhl/dot_general | solution.py:97
  74.8 0.0 copy-start.4
  74.8 0.0 copy-start.2
  74.9 0.8 copy.103
  75.7 0.0 all-to-all-done
  75.7 6.0 %all-to-all-start.1 = ((f32[4,8,8,512]{3,2,0,1:T(8,128)}), f32[4,8,8,512]{3,2,0,1:T(8,128)S(1)}, u32[]{:S(2)}, u32[]{:S(2)}) async-start(f32[4,8,8,512]{3,2,0,1:T(8,128)} %copy.103), calls=%async_computation.1 | async-start | bytes 1048576 | tf_op jit(solution)/shard_map/all_to_all | solution.py:113
  81.7 0.8 fusion.6
  82.5 0.5 fusion.3
  83.0 0.1 select_reduce_fusion.2
  83.1 3.4 %pmax.7 = f32[4,8,8]{2,1,0:T(8,128)S(1)} all-reduce(f32[4,8,8]{2,1,0:T(8,128)S(1)} %select_reduce_fusion.2), channel_id=1, replica_groups=mesh['grp'=2,'seq'=8,'head'=2] {'head'}, use_global_device_ids=true, to_apply=%region_12.13 | all-reduce | flops 256 | bytes 2048 | tf_op jit(solution)/shard_map/pmax | solution.py:73
  86.5 0.6 broadcast_select_fusion
  87.2 4.8 %all-to-all-done.1 = f32[4,8,8,512]{3,2,0,1:T(8,128)S(1)} async-done(((f32[4,8,8,512]{3,2,0,1:T(8,128)}), f32[4,8,8,512]{3,2,0,1:T(8,128)S(1)}, u32[]{:S(2)}, u32[]{:S(2)}) %all-to-all-start.1) | async-done | bytes 524320 | tf_op jit(solution)/shard_map/all_to_all | solution.py:113
  92.0 0.1 multiply_reduce_fusion
  92.1 0.1 divide_convert_fusion
  92.2 0.2 fusion.4
  92.4 0.6 copy.107
  (34 shorter events, 0.3 us)
Async XLA Ops:
  0.6 1.2 %copy-start = (bf16[8,128,512]{2,1,0:T(8,128)(2,1)S(1)}, bf16[8,128,512]{2,1,0:T(8,128)(2,1)}, u32[]{:S(2)}) copy-start(bf16[8,128,512]{2,1,0:T(8,128)(2,1)} %param.9) | copy-start | bytes 3145732
  4.1 15.6 %collective-permute-start = (bf16[4,8,576]{2,1,0:T(8,128)(2,1)}, bf16[4,8,576]{2,1,0:T(8,128)(2,1)S(1)}, u32[]{:S(2)}, u32[]{:S(2)}) collective-permute-start(bf16[4,8,576]{2,1,0:T(8,128)(2,1)} %pad_maximum_fusion), channel_id=1, source_target_pairs={{0,2},{2,4},{4,6},{6,8},{8,10},{10,12},{12,14},{14,0},{1,3},{3,5},... | collective-permute-start | bytes 110600 | tf_op jit(solution)/shard_map/ppermute | solution.py:16
  7.1 20.1 %collective-permute-start.4 = (bf16[4,8,576]{2,1,0:T(8,128)(2,1)}, bf16[4,8,576]{2,1,0:T(8,128)(2,1)S(1)}, u32[]{:S(2)}, u32[]{:S(2)}) collective-permute-start(bf16[4,8,576]{2,1,0:T(8,128)(2,1)} %pad_maximum_fusion), channel_id=1, source_target_pairs={{0,14},{2,0},{4,2},{6,4},{8,6},{10,8},{12,10},{14,12},{1,15},{3,1}... | collective-permute-start | bytes 110600 | tf_op jit(solution)/shard_map/ppermute | solution.py:18
  11.4 8.4 %copy-start.9 = (s32[4,8,32]{2,1,0:T(8,128)S(1)}, s32[4,8,32]{2,1,0:T(8,128)}, u32[]{:S(2)}) copy-start(s32[4,8,32]{2,1,0:T(8,128)} %param.13) | copy-start | bytes 12292
  15.7 26.9 %copy-start.6 = (bf16[4,8,64]{2,1,0:T(8,128)(2,1)S(1)}, bf16[4,8,64]{2,1,0:T(8,128)(2,1)}, u32[]{:S(2)}) copy-start(bf16[4,8,64]{2,1,0:T(8,128)(2,1)} %param.8) | copy-start | bytes 12292
  15.7 31.8 %copy-start.1 = (bf16[4,512,576]{1,2,0:T(8,128)(2,1)S(1)}, bf16[4,512,576]{1,2,0:T(8,128)(2,1)}, u32[]{:S(2)}) copy-start(bf16[4,512,576]{1,2,0:T(8,128)(2,1)} %param.11) | copy-start | bytes 7077892
  19.8 6.7 %collective-permute-start.1 = (bf16[4,8,576]{2,1,0:T(8,128)(2,1)S(1)}, bf16[4,8,576]{2,1,0:T(8,128)(2,1)S(1)}, u32[]{:S(2)}, u32[]{:S(2)}) collective-permute-start(bf16[4,8,576]{2,1,0:T(8,128)(2,1)S(1)} %collective-permute-done), channel_id=1, source_target_pairs={{0,2},{2,4},{4,6},{6,8},{8,10},{10,12},{12,14},{14,0},{1,3},{3,5},... | collective-permute-start | bytes 110600 | tf_op jit(solution)/shard_map/ppermute | solution.py:16
  26.5 0.8 copy-start.5
  26.5 6.8 %collective-permute-start.2 = (bf16[4,8,576]{2,1,0:T(8,128)(2,1)S(1)}, bf16[4,8,576]{2,1,0:T(8,128)(2,1)}, u32[]{:S(2)}, u32[]{:S(2)}) collective-permute-start(bf16[4,8,576]{2,1,0:T(8,128)(2,1)S(1)} %collective-permute-done.1), channel_id=1, source_target_pairs={{0,2},{2,4},{4,6},{6,8},{8,10},{10,12},{12,14},{14,0},{1,3},{3,5},... | collective-permute-start | bytes 110600 | tf_op jit(solution)/shard_map/ppermute | solution.py:16
  27.3 6.4 %collective-permute-start.5 = (bf16[4,8,576]{2,1,0:T(8,128)(2,1)S(1)}, bf16[4,8,576]{2,1,0:T(8,128)(2,1)}, u32[]{:S(2)}, u32[]{:S(2)}) collective-permute-start(bf16[4,8,576]{2,1,0:T(8,128)(2,1)S(1)} %collective-permute-done.4), channel_id=1, source_target_pairs={{0,14},{2,0},{4,2},{6,4},{8,6},{10,8},{12,10},{14,12},{1,15},{3,1}... | collective-permute-start | bytes 110600 | tf_op jit(solution)/shard_map/ppermute | solution.py:18
  33.3 7.0 %collective-permute-start.3 = (bf16[4,8,576]{2,1,0:T(8,128)(2,1)}, bf16[4,8,576]{2,1,0:T(8,128)(2,1)}, u32[]{:S(2)}, u32[]{:S(2)}) collective-permute-start(bf16[4,8,576]{2,1,0:T(8,128)(2,1)} %collective-permute-done.2), channel_id=1, source_target_pairs={{0,2},{2,4},{4,6},{6,8},{8,10},{10,12},{12,14},{14,0},{1,3},{3,5},... | collective-permute-start | bytes 110600 | tf_op jit(solution)/shard_map/ppermute | solution.py:16
  33.7 9.8 %collective-permute-start.6 = (bf16[4,8,576]{2,1,0:T(8,128)(2,1)}, bf16[4,8,576]{2,1,0:T(8,128)(2,1)S(1)}, u32[]{:S(2)}, u32[]{:S(2)}) collective-permute-start(bf16[4,8,576]{2,1,0:T(8,128)(2,1)} %collective-permute-done.5), channel_id=1, source_target_pairs={{0,14},{2,0},{4,2},{6,4},{8,6},{10,8},{12,10},{14,12},{1,15},{3,1}... | collective-permute-start | bytes 110600 | tf_op jit(solution)/shard_map/ppermute | solution.py:18
  46.7 0.8 copy-start.3
  51.9 10.1 %all-to-all-start.2 = ((f32[4,8,8]{2,0,1:T(4,128)}), f32[4,8,8]{2,0,1:T(4,128)S(1)}, u32[]{:S(2)}, u32[]{:S(2)}) async-start(f32[4,8,8]{2,0,1:T(4,128)} %copy.104), calls=%async_computation.2 | async-start | bytes 32768 | tf_op jit(solution)/shard_map/all_to_all | solution.py:106
  62.1 13.6 %all-to-all-start = ((f32[4,8,8]{2,0,1:T(4,128)}), f32[4,8,8]{2,0,1:T(4,128)S(1)}, u32[]{:S(2)}, u32[]{:S(2)}) async-start(f32[4,8,8]{2,0,1:T(4,128)} %copy.101), calls=%async_computation | async-start | bytes 32768 | tf_op jit(solution)/shard_map/all_to_all | solution.py:99
  74.8 6.9 %copy-start.4 = (bf16[4,128,576]{2,1,0:T(8,128)(2,1)S(1)}, bf16[4,128,576]{2,1,0:T(8,128)(2,1)}, u32[]{:S(2)}) copy-start(bf16[4,128,576]{2,1,0:T(8,128)(2,1)} %copy-done.3) | copy-start | bytes 1769476
  74.8 6.9 %copy-start.7 = (bf16[4,8,576]{2,1,0:T(8,128)(2,1)S(1)}, bf16[4,8,576]{2,1,0:T(8,128)(2,1)}, u32[]{:S(2)}) copy-start(bf16[4,8,576]{2,1,0:T(8,128)(2,1)} %get-tuple-element.18) | copy-start | bytes 110596
  74.8 6.9 %copy-start.8 = (bf16[4,8,576]{2,1,0:T(8,128)(2,1)S(1)}, bf16[4,8,576]{2,1,0:T(8,128)(2,1)}, u32[]{:S(2)}) copy-start(bf16[4,8,576]{2,1,0:T(8,128)(2,1)} %get-tuple-element.19) | copy-start | bytes 110596
  74.8 8.2 %copy-start.10 = (pred[8,64]{1,0:T(8,128)(4,1)S(1)}, pred[8,64]{1,0:T(8,128)(4,1)}, u32[]{:S(2)}) copy-start(pred[8,64]{1,0:T(8,128)(4,1)} %iota_compare_fusion) | copy-start | bytes 1540
  74.8 17.4 %copy-start.2 = (bf16[8,512,128]{2,1,0:T(8,128)(2,1)S(1)}, bf16[8,512,128]{2,1,0:T(8,128)(2,1)}, u32[]{:S(2)}) copy-start(bf16[8,512,128]{2,1,0:T(8,128)(2,1)} %param.10) | copy-start | bytes 3145732
  75.7 16.3 %all-to-all-start.1 = ((f32[4,8,8,512]{3,2,0,1:T(8,128)}), f32[4,8,8,512]{3,2,0,1:T(8,128)S(1)}, u32[]{:S(2)}, u32[]{:S(2)}) async-start(f32[4,8,8,512]{3,2,0,1:T(8,128)} %copy.103), calls=%async_computation.1 | async-start | bytes 1048576 | tf_op jit(solution)/shard_map/all_to_all | solution.py:113
